TPU v7x, 32 devices: a whole 2x2x4 slice. The times are simulated.
32 devices in a mesh: ctx: 16 (over z, x, core), head: 2 (over y).
Axes of the slice: x: 2, y: 2, z: 4, core: 2. Of those that a mesh axis runs over, the one named last changes fastest.
Arguments:
- features: float32 [4096, 8192], P(('ctx', 'head')), may hold values from -200 to 200
- state_write: float32 [4096, 1024], P(('ctx', 'head')), may hold values from -6 to 6
- state_read: float32 [4096, 1024], P(('ctx', 'head')), may hold values from -6 to 6
- log_decay: float32 [4096, 128], P(('ctx', 'head')), may hold values from -0.6932 to 0, as said below
- conv_features: float32 [4, 8192], replicated, may hold values from -3 to 3
- conv_write: float32 [4, 1024], replicated, may hold values from -3 to 3
- conv_read: float32 [4, 1024], replicated, may hold values from -3 to 3
- norm_gain: float32 [8192], P('head'), may hold values from 0.5 to 1.5
Outputs:
- normed_head_outputs: float32 [4096, 8192], P('ctx', 'head')
Inputs may be any that keep to these rules, and one draw needn't show every extreme that they name: `log_decay`: strictly negative.
All inputs are finite; a program needn't handle non-finite values.
Results may differ from a plain program's by a relative error of at most 0.00029.
Values sent between devices are 32-bit elements; how exact they have to be, the bound alone decides.
A program may use at most 128 MiB of HBM per device.

v0:
```python
import jax
import jax.numpy as jnp
from jax import lax
from jax.sharding import PartitionSpec as P

H = 128
P_SIZE = 64
N = 128
G = 8
BLOCK = 256
highest = lax.Precision.HIGHEST
eps_norm = 1e-05


def passed_along(value, axis, steps):
    count = lax.axis_size(axis)
    leading, last = (max(0, -steps), min(count, count - steps))
    return lax.ppermute(value, axis, [(source, source + steps) for source in range(leading, last)])


def causal_conv(tokens, leading, weight):
    tap_count = weight.shape[0]
    padded = jnp.concatenate([leading, tokens], 0)
    extent = tokens.shape[0]
    summed = weight[0] * padded[0:extent]
    for displacement in range(1, tap_count):
        summed = summed + weight[displacement] * padded[displacement : displacement + extent]
    return jax.nn.silu(summed)


def block_pass(carried_state, blocked):
    inputs_act, writes_act, reads_act, decays = blocked
    cumulative = jnp.cumsum(decays, 0)
    extent = decays.shape[0]
    target = lax.broadcasted_iota(jnp.int32, (extent, extent), 0)
    source = lax.broadcasted_iota(jnp.int32, (extent, extent), 1)
    strictly_past = target >= source
    along = jnp.transpose(cumulative, (1, 2, 0))
    spacing = jnp.where(strictly_past, along[..., :, None] - along[..., None, :], 0.0)
    damping = jnp.where(strictly_past, jnp.exp(spacing), 0.0)
    scores = jnp.einsum("tgn,sgn->gts", reads_act, writes_act, precision=highest)
    within_range = jnp.einsum(
        "ghts,sghp->tghp", scores[:, None] * damping, inputs_act, precision=highest
    )
    entering = (
        jnp.einsum("tgn,ghpn->tghp", reads_act, carried_state, precision=highest)
        * jnp.exp(cumulative)[..., None]
    )
    remaining = jnp.exp(cumulative[-1] - cumulative)
    new_state = jnp.exp(cumulative[-1])[..., None, None] * carried_state + jnp.einsum(
        "sgh,sghp,sgn->ghpn", remaining, inputs_act, writes_act, precision=highest
    )
    return (new_state, within_range + entering)


def split_rim(edges, first_width, second_width):
    return (
        edges[:, :first_width],
        edges[:, first_width : first_width + second_width],
        edges[:, first_width + second_width :],
    )


def shards(
    features, state_write, state_read, log_decay, conv_features, conv_write, conv_read, norm_gain
):
    tap_count = conv_features.shape[0]
    head_count = lax.axis_size("head")
    local_heads = H // head_count
    groups_here = G // head_count
    per_group = H // G
    moving = (features, state_write, state_read)
    inputs_act, writes_act, reads_act, decays = (
        lax.all_to_all(moving[0], "head", split_axis=1, concat_axis=0, tiled=True),
        lax.all_to_all(moving[1], "head", split_axis=1, concat_axis=0, tiled=True),
        lax.all_to_all(moving[2], "head", split_axis=1, concat_axis=0, tiled=True),
        lax.all_to_all(log_decay, "head", split_axis=1, concat_axis=0, tiled=True),
    )
    rim = jnp.concatenate(
        [
            inputs_act[-(tap_count - 1) :],
            writes_act[-(tap_count - 1) :],
            reads_act[-(tap_count - 1) :],
        ],
        1,
    )
    edges = passed_along(rim, "ctx", 1)
    lead_inputs, lead_writes, lead_reads = split_rim(
        edges, inputs_act.shape[1], writes_act.shape[1]
    )
    position = lax.axis_index("head")
    input_width = inputs_act.shape[1]
    state_width = writes_act.shape[1]
    inputs_act = causal_conv(
        inputs_act,
        lead_inputs,
        lax.dynamic_slice_in_dim(conv_features, position * input_width, input_width, 1),
    )
    writes_act = causal_conv(
        writes_act,
        lead_writes,
        lax.dynamic_slice_in_dim(conv_write, position * state_width, state_width, 1),
    )
    reads_act = causal_conv(
        reads_act,
        lead_reads,
        lax.dynamic_slice_in_dim(conv_read, position * state_width, state_width, 1),
    )
    length = inputs_act.shape[0]
    blocks = length // BLOCK
    blocked = (
        inputs_act.reshape(blocks, BLOCK, groups_here, per_group, P_SIZE),
        writes_act.reshape(blocks, BLOCK, groups_here, N),
        reads_act.reshape(blocks, BLOCK, groups_here, N),
        decays.reshape(blocks, BLOCK, groups_here, per_group),
    )
    initial = jnp.zeros((groups_here, per_group, P_SIZE, N), jnp.float32)
    final_state, partial_value = lax.scan(block_pass, initial, blocked)
    within = partial_value.reshape(length, groups_here, per_group, P_SIZE)
    decay_groups = decays.reshape(length, groups_here, per_group)
    segment_log = jnp.sum(decay_groups, 0)
    flattened = final_state.reshape(1, local_heads, P_SIZE * N)
    pieces = lax.all_to_all(flattened, "ctx", split_axis=2, concat_axis=0, tiled=True)
    totals = lax.all_gather(segment_log.reshape(1, local_heads), "ctx", axis=0, tiled=True)
    running = jnp.cumsum(totals, 0)
    segments = totals.shape[0]
    target = lax.broadcasted_iota(jnp.int32, (segments, segments), 0)
    source = lax.broadcasted_iota(jnp.int32, (segments, segments), 1)
    before = (source < target)[..., None]
    spacing = jnp.where(before, (running - totals)[:, None, :] - running[None, :, :], 0.0)
    weight = jnp.where(before, jnp.exp(spacing), 0.0)
    prefix = jnp.einsum("cdh,dhq->chq", weight, pieces, precision=highest)
    returned = lax.all_to_all(prefix, "ctx", split_axis=0, concat_axis=2, tiled=True)
    incoming = returned.reshape(groups_here, per_group, P_SIZE, N)
    rising = jnp.exp(jnp.cumsum(decay_groups, 0))
    carried = (
        jnp.einsum(
            "tgn,ghpn->tghp", reads_act.reshape(length, groups_here, N), incoming, precision=highest
        )
        * rising[..., None]
    )
    mixed = (within + carried).reshape(length, groups_here, per_group * P_SIZE)
    inverse = lax.rsqrt(jnp.mean(mixed * mixed, -1, keepdims=True) + eps_norm)
    return (mixed * inverse).reshape(length, local_heads * P_SIZE) * norm_gain


def solution(mesh):
    return jax.shard_map(
        shards,
        mesh=mesh,
        in_specs=(
            P(("ctx", "head"), None),
            P(("ctx", "head"), None),
            P(("ctx", "head"), None),
            P(("ctx", "head"), None),
            P(),
            P(),
            P(),
            P("head"),
        ),
        out_specs=P("ctx", "head"),
        check_vma=False,
    )
```

profile of v0, /device:TPU:11, one launch (start us, length us, event | category | flops | bytes accessed | tf_op | source)
XLA Modules:
  0.0 362.2 jit_solution(3611909566729080655)
XLA Ops:
  0.0 1.6 copy.62
  1.6 3.3 all-to-all-start.3
  4.9 2.0 copy.53
  6.9 0.9 all-to-all-done.3
  7.8 3.5 all-to-all-start.1
  11.3 2.0 copy.55
  13.3 4.2 %all-to-all-done.1 = f32[128,2,512]{0,2,1:T(8,128)S(1)} async-done(((f32[128,2,512]{0,2,1:T(8,128)}), f32[128,2,512]{0,2,1:T(8,128)S(1)}, u32[]{:S(2)}, u32[]{:S(2)}) %all-to-all-start.1) | async-done | bytes 524320 | tf_op jit(solution)/shard_map/all_to_all | solution.py:75
  17.5 3.5 all-to-all-start.2
  21.0 5.6 %copy.51 = f32[128,8192]{0,1:T(8,128)} copy(f32[128,8192]{1,0:T(8,128)} %param.8) | data formatting | bytes 8388608 | tf_op args[0]
  26.6 5.8 %all-to-all-start = ((f32[128,2,4096]{0,2,1:T(8,128)}), f32[128,2,4096]{0,2,1:T(8,128)}, u32[]{:S(2)}, u32[]{:S(2)}) async-start(f32[128,2,4096]{0,2,1:T(8,128)} %bitcast.110), calls=%async_computation | async-start | bytes 8388608 | tf_op jit(solution)/shard_map/all_to_all | solution.py:74
  32.4 0.1 constant_dynamic-slice_fusion.1
  32.6 0.2 constant_dynamic-slice_fusion
  32.7 0.1 copy.63
  32.8 0.1 squeeze.26
  32.9 2.3 reduce-window.12
  35.2 0.2 slice_reduce_fusion
  35.4 0.1 bitcast_bitcast_fusion.1
  35.5 0.2 slice_reduce_fusion.1
  35.6 0.1 fusion.63
  35.7 0.2 copy.54
  35.9 0.2 copy.56
  36.2 40.1 %all-to-all-done = f32[128,2,4096]{0,2,1:T(8,128)} async-done(((f32[128,2,4096]{0,2,1:T(8,128)}), f32[128,2,4096]{0,2,1:T(8,128)}, u32[]{:S(2)}, u32[]{:S(2)}) %all-to-all-start) | async-done | bytes 4194336 | tf_op jit(solution)/shard_map/all_to_all | solution.py:74
  76.2 5.6 %copy.52 = f32[2,128,4096]{2,1,0:T(8,128)} copy(f32[2,128,4096]{1,2,0:T(8,128)} %bitcast.2) | data formatting | bytes 8388608 | tf_op jit(solution)/shard_map/all_to_all | solution.py:74
  81.8 0.9 slice.124
  82.8 8.1 %collective-permute-start = (f32[3,5120]{1,0:T(4,128)S(1)}, f32[3,5120]{1,0:T(4,128)S(1)}, u32[]{:S(2)}, u32[]{:S(2)}) collective-permute-start(f32[3,5120]{1,0:T(4,128)S(1)} %pad_maximum_fusion.3), channel_id=1, source_target_pairs={{0,2},{2,4},{4,6},{6,8},{8,10},{10,12},{12,14},{14,16},{16,18},{18... | collective-permute-start | bytes 184328 | tf_op jit(solution)/shard_map/ppermute | solution.py:18
  90.9 0.9 collective-permute-done
  91.8 0.3 divide_multiply_fusion.1
  92.2 0.2 copy.59
  92.4 8.9 %divide_multiply_fusion = f32[256,4096]{1,0:T(8,128)} fusion(f32[256,4096]{1,0:T(8,128)} %bitcast.106, f32[3,4096]{1,0:T(4,128)S(1)} %slice.127, f32[4096]{0:T(1024)S(1)} %bitcast.131, f32[4096]{0:T(1024)S(1)} %bitcast.129, f32[4096]{0:T(1024)S(1)} %bitcast.130, f32[4096]{0:T(1024)S(1)} %bitcast.128), kind=kLoop, calls=%fused_computation.30 | loop fusion | flops 14680064 | bytes 8503296 | tf_op jit(solution)/shard_map/jit(silu)/mul | solution.py:28
  101.3 5.6 %copy.57 = f32[256,4096]{0,1:T(8,128)} copy(f32[256,4096]{1,0:T(8,128)} %divide_multiply_fusion) | data formatting | bytes 8388608 | tf_op jit(solution)/shard_map/jit(silu)/mul | solution.py:28
  106.9 7.3 %fusion.28 = f32[4,16,64,128]{3,2,1,0:T(8,128)} fusion(f32[256,4,128,1]{0,2,3,1:T(8,128)S(1)} %bitcast.118, f32[256,4,16,64]{0,3,2,1:T(8,128)} %bitcast.107, f32[256,4,16]{0,2,1:T(8,128)S(1)} %get-tuple-element.33, f32[4,16]{1,0:T(4,128)S(1)} %exponential_multiply_fusion), kind=kOutput, calls=%fused_computation.34 | convolution fusion | flops 1612185600 | bytes 6881536 | tf_op jit(solution)/shard_map/while/body/eval_jaxpr/sgh,sghp,sgn->ghpn/dot_general | solution.py:50
  114.2 1.7 reshape.89
  115.9 6.6 %copy.68 = f32[1,64,8192]{1,0,2:T(1,128)} copy(f32[1,64,8192]{2,1,0:T(8,128)S(1)} %reshape.89) | data formatting | bytes 4194304 | tf_op jit(solution)/shard_map/reshape | solution.py:122
  122.5 0.5 broadcast.41
  123.0 38.3 %reduce.7 = f32[8192,64]{1,0:T(8,128)} reduce(f32[8192,1,64]{2,1,0:T(1,128)} %bitcast.112, f32[]{:T(128)} %broadcast.41), dimensions={1}, to_apply=%bitcast.91.reduce_sub_computation | reduce | bytes 4194308
  161.3 5.5 %reshape.104 = f32[16,1,32768]{2,1,0:T(1,128)} reshape(f32[8192,64]{1,0:T(8,128)} %reduce.7) | data formatting | bytes 4194304
  166.9 7.1 %all-to-all-start.4 = ((f32[16,1,32768]{2,1,0:T(1,128)}), f32[16,1,32768]{2,1,0:T(1,128)}, u32[]{:S(2)}, u32[]{:S(2)}) async-start(f32[16,1,32768]{2,1,0:T(1,128)} %reshape.104), calls=%async_computation.4 | async-start | bytes 4194304 | tf_op jit(solution)/shard_map/all_to_all | solution.py:123
  173.9 0.6 dynamic-slice
  175.2 0.1 reduce_sum.18
  175.3 0.2 dynamic-update-slice
  175.5 62.4 %all-reduce = f32[1024]{0:T(1024)S(1)} all-reduce(f32[1024]{0:T(1024)S(1)} %dynamic-update-slice), channel_id=2, replica_groups=mesh['ctx'=16,'head'=2] {'ctx'}, use_global_device_ids=true, to_apply=%add | all-reduce | flops 1024 | bytes 8192
  238.0 0.1 reshape.93
  238.1 0.1 copy.71
  238.2 0.1 copy.70
  238.2 7.2 %reduce.8 = f32[16,32768]{1,0:T(8,128)S(1)} reduce(f32[16,1,32768]{2,1,0:T(1,128)} %all-to-all-done.4, f32[]{:T(128)} %broadcast.41), dimensions={1}, to_apply=%all_to_all.93.reduce_sub_computation | reduce | bytes 4194308 | tf_op jit(solution)/shard_map/all_to_all | solution.py:123
  245.5 6.6 %reshape.105 = f32[8192,1,64]{2,1,0:T(1,128)} reshape(f32[16,32768]{1,0:T(8,128)S(1)} %reduce.8) | data formatting | bytes 4194304
  252.0 3.4 copy.86
  255.4 2.1 fusion.31
  257.5 2.5 copy.72
  260.0 5.9 %all-to-all-start.5 = ((f32[16,64,512]{2,1,0:T(8,128)}), f32[16,64,512]{2,1,0:T(8,128)S(1)}, u32[]{:S(2)}, u32[]{:S(2)}) async-start(f32[16,64,512]{2,1,0:T(8,128)} %copy.72), calls=%async_computation.5 | async-start | bytes 4194304 | tf_op jit(solution)/shard_map/all_to_all | solution.py:133
  266.0 1.1 divide_multiply_fusion.2
  267.1 1.2 copy.58
  268.3 2.0 fusion.66
  270.4 4.9 %fusion.34 = f32[4,16,64,256]{3,2,1,0:T(8,128)} fusion(f32[256,4,128,1]{0,2,3,1:T(8,128)S(1)} %bitcast.116), kind=kOutput, calls=%fused_computation.36 | convolution fusion | flops 1610612736 | bytes 4718592 | tf_op jit(solution)/shard_map/while/body/eval_jaxpr/tgn,ghpn->tghp/dot_general | solution.py:46
  275.3 38.1 %all-to-all-done.5 = f32[16,64,512]{2,1,0:T(8,128)S(1)} async-done(((f32[16,64,512]{2,1,0:T(8,128)}), f32[16,64,512]{2,1,0:T(8,128)S(1)}, u32[]{:S(2)}, u32[]{:S(2)}) %all-to-all-start.5) | async-done | bytes 2097184 | tf_op jit(solution)/shard_map/all_to_all | solution.py:133
  313.4 2.5 copy.73
  315.9 1.6 reshape.91
  317.6 3.4 fusion.67
  321.0 22.4 %multiply_reduce_fusion = (f32[256,4]{0,1:T(4,128)S(1)}, f32[256,4,16,64]{0,3,2,1:T(8,128)}) fusion(f32[4,16,64,256]{3,2,1,0:T(8,128)S(1)} %fusion.67, f32[256,4,16]{0,2,1:T(8,128)S(1)} %get-tuple-element.32, f32[4,16,64,256]{3,2,1,0:T(8,128)} %fusion.34, f32[256,4,16,64]{0,3,2,1:T(8,128)S(1)} %bitcast.108, f32[4,16,256]{2,1,0:T(8,128)S(1)} %get-tuple-element.34, ...), kind=kOutput, calls=%fused_computation.27 | convolution fusion | flops 3244293120 | bytes 18026496 | tf_op jit(solution)/shard_map/while/body/eval_jaxpr/ghts,sghp->tghp/dot_general | solution.py:42
  343.4 0.1 copy.75
  343.6 0.6 mul.253
  344.2 5.8 %copy.91 = f32[32,8,4,1024]{3,1,2,0:T(8,128)} copy(f32[32,8,4,1024]{3,2,1,0:T(4,128)S(1)} %bitcast.113) | data formatting | bytes 8388608
  349.9 5.6 %copy.76 = f32[256,4096]{1,0:T(8,128)} copy(f32[256,4096]{0,1:T(8,128)} %bitcast.120) | data formatting | bytes 8388608 | tf_op jit(solution)/shard_map/reshape | solution.py:142
  355.6 6.3 %multiply_multiply_fusion = f32[256,4096]{1,0:T(8,128)} fusion(f32[256,4096]{1,0:T(8,128)} %copy.76, f32[256,4096]{1,0:T(8,128)} %bitcast.111, f32[4096]{0:T(1024)S(1)} %copy-done.3), kind=kLoop, calls=%fused_computation.26 | loop fusion | flops 2097152 | bytes 12599296 | tf_op jit(solution)/shard_map/mul | solution.py:144
  (31 shorter events, 0.2 us)
Async XLA Ops:
  1.6 6.3 %all-to-all-start.3 = ((f32[128,2,64]{0,2,1:T(8,128)}), f32[128,2,64]{0,2,1:T(8,128)S(1)}, u32[]{:S(2)}, u32[]{:S(2)}) async-start(f32[128,2,64]{0,2,1:T(8,128)} %bitcast.24), calls=%async_computation.3 | async-start | bytes 131072 | tf_op jit(solution)/shard_map/all_to_all | solution.py:77
  7.8 9.7 %all-to-all-start.1 = ((f32[128,2,512]{0,2,1:T(8,128)}), f32[128,2,512]{0,2,1:T(8,128)S(1)}, u32[]{:S(2)}, u32[]{:S(2)}) async-start(f32[128,2,512]{0,2,1:T(8,128)} %bitcast.4), calls=%async_computation.1 | async-start | bytes 1048576 | tf_op jit(solution)/shard_map/all_to_all | solution.py:75
  17.5 9.1 %all-to-all-start.2 = ((f32[128,2,512]{0,2,1:T(8,128)}), f32[128,2,512]{0,2,1:T(8,128)S(1)}, u32[]{:S(2)}, u32[]{:S(2)}) async-start(f32[128,2,512]{0,2,1:T(8,128)} %bitcast.7), calls=%async_computation.2 | async-start | bytes 1048576 | tf_op jit(solution)/shard_map/all_to_all | solution.py:76
  26.6 5.8 %copy-start.4 = (f32[4,1024]{1,0:T(4,128)S(1)}, f32[4,1024]{1,0:T(4,128)}, u32[]{:S(2)}) copy-start(f32[4,1024]{1,0:T(4,128)} %param.14) | copy-start | bytes 49156
  26.6 5.8 %copy-start.5 = (f32[4,1024]{1,0:T(4,128)S(1)}, f32[4,1024]{1,0:T(4,128)}, u32[]{:S(2)}) copy-start(f32[4,1024]{1,0:T(4,128)} %param.13) | copy-start | bytes 49156
  26.6 5.9 %copy-start.2 = (f32[4,8192]{1,0:T(4,128)S(1)}, f32[4,8192]{1,0:T(4,128)}, u32[]{:S(2)}) copy-start(f32[4,8192]{1,0:T(4,128)} %param.12) | copy-start | bytes 393220
  26.6 49.6 %all-to-all-start = ((f32[128,2,4096]{0,2,1:T(8,128)}), f32[128,2,4096]{0,2,1:T(8,128)}, u32[]{:S(2)}, u32[]{:S(2)}) async-start(f32[128,2,4096]{0,2,1:T(8,128)} %bitcast.110), calls=%async_computation | async-start | bytes 8388608 | tf_op jit(solution)/shard_map/all_to_all | solution.py:74
  82.8 9.0 %collective-permute-start = (f32[3,5120]{1,0:T(4,128)S(1)}, f32[3,5120]{1,0:T(4,128)S(1)}, u32[]{:S(2)}, u32[]{:S(2)}) collective-permute-start(f32[3,5120]{1,0:T(4,128)S(1)} %pad_maximum_fusion.3), channel_id=1, source_target_pairs={{0,2},{2,4},{4,6},{6,8},{8,10},{10,12},{12,14},{14,16},{16,18},{18... | collective-permute-start | bytes 184328 | tf_op jit(solution)/shard_map/ppermute | solution.py:18
  161.3 12.6 %copy-start.6 = (u32[32]{0:T(128)S(1)}, u32[32]{0:T(128)}, u32[]{:S(2)}) copy-start(u32[32]{0:T(128)} %constant.53) | copy-start | bytes 388
  166.9 71.4 %all-to-all-start.4 = ((f32[16,1,32768]{2,1,0:T(1,128)}), f32[16,1,32768]{2,1,0:T(1,128)}, u32[]{:S(2)}, u32[]{:S(2)}) async-start(f32[16,1,32768]{2,1,0:T(1,128)} %reshape.104), calls=%async_computation.4 | async-start | bytes 4194304 | tf_op jit(solution)/shard_map/all_to_all | solution.py:123
  260.0 53.3 %all-to-all-start.5 = ((f32[16,64,512]{2,1,0:T(8,128)}), f32[16,64,512]{2,1,0:T(8,128)S(1)}, u32[]{:S(2)}, u32[]{:S(2)}) async-start(f32[16,64,512]{2,1,0:T(8,128)} %copy.72), calls=%async_computation.5 | async-start | bytes 4194304 | tf_op jit(solution)/shard_map/all_to_all | solution.py:133
  317.6 3.5 copy-start
  317.6 3.5 copy-start.1
  349.9 5.6 %copy-start.3 = (f32[4096]{0:T(1024)S(1)}, f32[4096]{0:T(1024)}, u32[]{:S(2)}) copy-start(f32[4096]{0:T(1024)} %param.15) | copy-start | bytes 49156
where the time goes:
time: 366 us; the launch traced here: 362 us
  waiting for transfers between devices  84.2 us (23%)
  local copies, waits for them, and re-layouts  70.1 us (19%)
  other arithmetic  64.9 us (18%)
  blocking collectives  62.4 us (17%)
  matrix products  42.1 us (12%)
  starting transfers between devices  37.1 us (10%)
    unnamed x1, blocking collectives  62.4 us
    all_to_all x1, waiting for transfers between devices, shards(): lax.all_to_all(moving[0], 'head', split_axis=1, concat_axis=0, tiled=True)  40.1 us
    unnamed x1, other arithmetic  38.3 us
    all_to_all x1, waiting for transfers between devices, shards(): lax.all_to_all(prefix, 'ctx', split_axis=0, concat_axis=2, tiled=True)  38.1 us
    unnamed x25, local copies, waits for them, and re-layouts  30.4 us
    dot_general x1, matrix products, block_pass(): jnp.einsum('ghts,sghp->tghp', scores[:, None] * damping, inputs_act, prec...  22.4 us
    mul x3, other arithmetic, causal_conv(): return jax.nn.silu(summed)  10.3 us
    reshape x2, local copies, waits for them, and re-layouts, shards(): flattened = final_state.reshape(1, local_heads, P_SIZE * N)  8.32 us
  transfers between devices with their start and end apart: 7, of which 5 were waited for; matrix products, arithmetic and copies ran while one was open for 7% of the time, Pallas kernels for 0%

commit v1 on v0

--- a/solution.py
+++ b/solution.py
@@ -10,6 +10,18 @@
 BLOCK = 256
 highest = lax.Precision.HIGHEST
 eps_norm = 1e-05
+
+
+def cut_along(array, dim, size):
+    dims = array.shape
+    blocks = array.reshape(*dims[:dim], size, dims[dim] // size, *dims[dim + 1 :])
+    return jnp.moveaxis(blocks, dim, 0)
+
+
+def laid_out(blocks, dim):
+    shape = list(blocks.shape[1:])
+    shape[dim] *= blocks.shape[0]
+    return jnp.moveaxis(blocks, 0, dim).reshape(shape)
 
 
 def passed_along(value, axis, steps):
@@ -130,7 +142,15 @@
     spacing = jnp.where(before, (running - totals)[:, None, :] - running[None, :, :], 0.0)
     weight = jnp.where(before, jnp.exp(spacing), 0.0)
     prefix = jnp.einsum("cdh,dhq->chq", weight, pieces, precision=highest)
-    returned = lax.all_to_all(prefix, "ctx", split_axis=0, concat_axis=2, tiled=True)
+    peers, index = (lax.axis_size("ctx"), lax.axis_index("ctx"))
+    blocks_2 = cut_along(prefix, 0, peers)
+    result = blocks_2
+    for lap in range(1, peers):
+        target_2, source_2 = ((index + lap) % peers, (index - lap) % peers)
+        sent = lax.dynamic_index_in_dim(blocks_2, target_2, 0)
+        other = lax.ppermute(sent, "ctx", [(i, (i + lap) % peers) for i in range(peers)])
+        result = lax.dynamic_update_slice_in_dim(result, other, source_2, axis=0)
+    returned = laid_out(result, 2)
     incoming = returned.reshape(groups_here, per_group, P_SIZE, N)
     rising = jnp.exp(jnp.cumsum(decay_groups, 0))
     carried = (

time: 366 us -> 403 us (1.10)
  starting transfers between devices: 37.1 us -> 75.8 us
  waiting for transfers between devices: 84.2 us -> 52 us
  local copies, waits for them, and re-layouts: 70.1 us -> 96 us
  matrix products: 42.1 us -> 47.5 us
    all_to_all x1 -> x0, waiting for transfers between devices: 38.1 us -> none  [shards(): lax.all_to_all(prefix, 'ctx', split_axis=0, concat_axis=2, tiled=True)]
    ppermute x0 -> x15, starting transfers between devices: none -> 30.7 us  [shards(): lax.ppermute(sent, 'ctx', [(i, (i + lap) % peers) for i in range(peers)])]
    dynamic_update_slice x0 -> x15, local copies, waits for them, and re-layouts: none -> 30.3 us  [shards(): result = lax.dynamic_update_slice_in_dim(result, other, source_2, axis=0)]
    all_to_all x1, starting transfers between devices: 7.07 us -> 21.1 us  [shards(): lax.all_to_all(flattened, 'ctx', split_axis=2, concat_axis=0, tiled=True)]
    dot_general x1, matrix products: 3.44 us -> 10.2 us  [shards(): jnp.einsum('tgn,ghpn->tghp', reads_act.reshape(length, groups_here, N), i...]
    ppermute x0 -> x15, waiting for transfers between devices: none -> 6.37 us  [shards(): lax.ppermute(sent, 'ctx', [(i, (i + lap) % peers) for i in range(peers)])]
    all_to_all x1 -> x0, starting transfers between devices: 5.93 us -> none  [shards(): lax.all_to_all(prefix, 'ctx', split_axis=0, concat_axis=2, tiled=True)]
    unnamed x25 -> x57, local copies, waits for them, and re-layouts: 30.4 us -> 28.6 us
  transfers between devices with their start and end apart: 7 -> 21, of which waited for: 5 -> 6; matrix products, arithmetic and copies ran while one was open for 7% -> 18% of each run, Pallas kernels for 0% -> 0%
where the time goes in v1:
time: 403 us; the launch traced here: 396 us
  local copies, waits for them, and re-layouts  96 us (24%)
  starting transfers between devices  75.8 us (19%)
  other arithmetic  61.7 us (15%)
  blocking collectives  61 us (15%)
  waiting for transfers between devices  52 us (13%)
  matrix products  47.5 us (12%)
    unnamed x1, blocking collectives  61 us
    all_to_all x1, waiting for transfers between devices, shards(): lax.all_to_all(moving[0], 'head', split_axis=1, concat_axis=0, tiled=True)  39.5 us
    unnamed x1, other arithmetic  38.4 us
    ppermute x15, starting transfers between devices, shards(): lax.ppermute(sent, 'ctx', [(i, (i + lap) % peers) for i in range(peers)])  30.7 us
    dynamic_update_slice x15, local copies, waits for them, and re-layouts, shards(): result = lax.dynamic_update_slice_in_dim(result, other, source_2, axis=0)  30.3 us
    unnamed x57, local copies, waits for them, and re-layouts  28.6 us
    all_to_all x1, starting transfers between devices, shards(): lax.all_to_all(flattened, 'ctx', split_axis=2, concat_axis=0, tiled=True)  21.1 us
    dot_general x1, matrix products, block_pass(): jnp.einsum('ghts,sghp->tghp', scores[:, None] * damping, inputs_act, prec...  20.1 us
  transfers between devices with their start and end apart: 21, of which 6 were waited for; matrix products, arithmetic and copies ran while one was open for 18% of the time, Pallas kernels for 0%

profile of v1, /device:TPU:11, one launch (start us, length us, event | category | flops | bytes accessed | tf_op | source)
XLA Modules:
  0.0 396.2 jit_solution(7598066878875104426)
XLA Ops:
  0.0 1.6 copy.62
  1.6 3.3 all-to-all-start.3
  4.9 2.0 copy.53
  6.9 0.9 all-to-all-done.3
  7.8 3.5 all-to-all-start.1
  11.3 2.0 copy.55
  13.4 4.2 %all-to-all-done.1 = f32[128,2,512]{0,2,1:T(8,128)S(1)} async-done(((f32[128,2,512]{0,2,1:T(8,128)}), f32[128,2,512]{0,2,1:T(8,128)S(1)}, u32[]{:S(2)}, u32[]{:S(2)}) %all-to-all-start.1) | async-done | bytes 524320 | tf_op jit(solution)/shard_map/all_to_all | solution.py:87
  17.6 3.5 all-to-all-start.2
  21.1 5.6 %copy.51 = f32[128,8192]{0,1:T(8,128)} copy(f32[128,8192]{1,0:T(8,128)} %param.8) | data formatting | bytes 8388608 | tf_op args[0]
  26.6 5.7 %all-to-all-start = ((f32[128,2,4096]{0,2,1:T(8,128)}), f32[128,2,4096]{0,2,1:T(8,128)}, u32[]{:S(2)}, u32[]{:S(2)}) async-start(f32[128,2,4096]{0,2,1:T(8,128)} %bitcast.139), calls=%async_computation | async-start | bytes 8388608 | tf_op jit(solution)/shard_map/all_to_all | solution.py:86
  32.9 2.3 reduce-window.12
  36.8 39.5 %all-to-all-done = f32[128,2,4096]{0,2,1:T(8,128)} async-done(((f32[128,2,4096]{0,2,1:T(8,128)}), f32[128,2,4096]{0,2,1:T(8,128)}, u32[]{:S(2)}, u32[]{:S(2)}) %all-to-all-start) | async-done | bytes 4194336 | tf_op jit(solution)/shard_map/all_to_all | solution.py:86
  76.2 5.6 %copy.52 = f32[2,128,4096]{2,1,0:T(8,128)} copy(f32[2,128,4096]{1,2,0:T(8,128)} %bitcast.2) | data formatting | bytes 8388608 | tf_op jit(solution)/shard_map/all_to_all | solution.py:86
  81.8 0.9 slice.124
  82.8 8.0 %collective-permute-start = (f32[3,5120]{1,0:T(4,128)S(1)}, f32[3,5120]{1,0:T(4,128)S(1)}, u32[]{:S(2)}, u32[]{:S(2)}) collective-permute-start(f32[3,5120]{1,0:T(4,128)S(1)} %pad_maximum_fusion.3), channel_id=1, source_target_pairs={{0,2},{2,4},{4,6},{6,8},{8,10},{10,12},{12,14},{14,16},{16,18},{18... | collective-permute-start | bytes 184328 | tf_op jit(solution)/shard_map/ppermute | solution.py:30
  90.8 1.0 collective-permute-done
  91.8 8.9 %divide_multiply_fusion = f32[256,4096]{1,0:T(8,128)} fusion(f32[256,4096]{1,0:T(8,128)} %bitcast.135, f32[3,4096]{1,0:T(4,128)S(1)} %slice.127, f32[4096]{0:T(1024)S(1)} %bitcast.159, f32[4096]{0:T(1024)S(1)} %bitcast.157, f32[4096]{0:T(1024)S(1)} %bitcast.158, f32[4096]{0:T(1024)S(1)} %bitcast.156), kind=kLoop, calls=%fused_computation.30 | loop fusion | flops 14680064 | bytes 8503296 | tf_op jit(solution)/shard_map/jit(silu)/mul | solution.py:40
  100.7 5.6 %copy.57 = f32[256,4096]{0,1:T(8,128)} copy(f32[256,4096]{1,0:T(8,128)} %divide_multiply_fusion) | data formatting | bytes 8388608 | tf_op jit(solution)/shard_map/jit(silu)/mul | solution.py:40
  106.9 7.3 %fusion.26 = f32[4,16,64,128]{3,2,1,0:T(8,128)} fusion(f32[256,4,128,1]{0,2,3,1:T(8,128)S(1)} %bitcast.147, f32[256,4,16,64]{0,3,2,1:T(8,128)} %bitcast.136, f32[256,4,16]{0,2,1:T(8,128)S(1)} %get-tuple-element.48, f32[4,16]{1,0:T(4,128)S(1)} %exponential_multiply_fusion), kind=kOutput, calls=%fused_computation.34 | convolution fusion | flops 1612185600 | bytes 6881536 | tf_op jit(solution)/shard_map/while/body/eval_jaxpr/sgh,sghp,sgn->ghpn/dot_general | solution.py:62
  114.1 1.7 reshape.133
  115.9 6.6 %copy.68 = f32[1,64,8192]{1,0,2:T(1,128)} copy(f32[1,64,8192]{2,1,0:T(8,128)S(1)} %reshape.133) | data formatting | bytes 4194304 | tf_op jit(solution)/shard_map/reshape | solution.py:134
  123.0 38.4 %reduce.7 = f32[8192,64]{1,0:T(8,128)} reduce(f32[8192,1,64]{2,1,0:T(1,128)} %bitcast.140, f32[]{:T(128)} %broadcast.71), dimensions={1}, to_apply=%bitcast.118.reduce_sub_computation | reduce | bytes 4194308
  161.3 5.5 %reshape.148 = f32[16,1,32768]{2,1,0:T(1,128)} reshape(f32[8192,64]{1,0:T(8,128)} %reduce.7) | data formatting | bytes 4194304
  166.8 21.1 %all-to-all-start.4 = ((f32[16,1,32768]{2,1,0:T(1,128)}), f32[16,1,32768]{2,1,0:T(1,128)}, u32[]{:S(2)}, u32[]{:S(2)}) async-start(f32[16,1,32768]{2,1,0:T(1,128)} %reshape.148), calls=%async_computation.4 | async-start | bytes 4194304 | tf_op jit(solution)/shard_map/all_to_all | solution.py:135
  190.8 61.0 %all-reduce = f32[1024]{0:T(1024)S(1)} all-reduce(f32[1024]{0:T(1024)S(1)} %dynamic-update-slice), channel_id=2, replica_groups=mesh['ctx'=16,'head'=2] {'ctx'}, use_global_device_ids=true, to_apply=%add | all-reduce | flops 1024 | bytes 8192
  252.7 7.2 %reduce.8 = f32[16,32768]{1,0:T(8,128)S(1)} reduce(f32[16,1,32768]{2,1,0:T(1,128)} %all-to-all-done.4, f32[]{:T(128)} %broadcast.71), dimensions={1}, to_apply=%all_to_all.82.reduce_sub_computation | reduce | bytes 4194308 | tf_op jit(solution)/shard_map/all_to_all | solution.py:135
  259.8 6.6 %reshape.149 = f32[8192,1,64]{2,1,0:T(1,128)} reshape(f32[16,32768]{1,0:T(8,128)S(1)} %reduce.8) | data formatting | bytes 4194304
  266.4 4.2 %copy.84 = f32[1,64,16,512]{3,2,1,0:T(8,128)} copy(f32[1,64,16,512]{1,3,2,0:T(8,128)} %bitcast.138) | data formatting | bytes 4194304 | tf_op jit(solution)/shard_map/all_to_all | solution.py:135
  270.6 3.8 fusion.23
  274.4 2.8 dynamic-slice_bitcast_fusion
  277.2 3.0 collective-permute-start.9
  280.1 1.4 collective-permute-start.8
  282.4 2.7 collective-permute-start.6
  285.1 1.0 fusion.61
  286.9 2.1 collective-permute-done.9
  289.0 1.3 collective-permute-start.4
  290.3 4.2 %collective-permute-done.8 = f32[1,1,64,512]{3,0,2,1:T(1,128)S(1)} collective-permute-done((f32[1,1,64,512]{3,0,2,1:T(1,128)S(1)}, f32[1,1,64,512]{3,0,2,1:T(1,128)S(1)}, u32[]{:S(2)}, u32[]{:S(2)}) %collective-permute-start.8) | collective-permute-done | bytes 131104 | tf_op jit(solution)/shard_map/ppermute | solution.py:151
  294.5 4.5 %collective-permute-start.3 = (f32[1,1,64,512]{3,0,2,1:T(1,128)S(1)}, f32[1,1,64,512]{3,0,2,1:T(1,128)S(1)}, u32[]{:S(2)}, u32[]{:S(2)}) collective-permute-start(f32[1,1,64,512]{3,0,2,1:T(1,128)S(1)} %get-tuple-element.38), channel_id=1, source_target_pairs={{0,6},{2,8},{4,10},{6,12},{8,14},{10,16},{12,18},{14,20},{16,22},{... | collective-permute-start | bytes 393224 | tf_op jit(solution)/shard_map/ppermute | solution.py:151
  298.9 7.2 %collective-permute-start.2 = (f32[1,1,64,512]{3,0,2,1:T(1,128)S(1)}, f32[1,1,64,512]{3,0,2,1:T(1,128)S(1)}, u32[]{:S(2)}, u32[]{:S(2)}) collective-permute-start(f32[1,1,64,512]{3,0,2,1:T(1,128)S(1)} %get-tuple-element.39), channel_id=1, source_target_pairs={{0,4},{2,6},{4,8},{6,10},{8,12},{10,14},{12,16},{14,18},{16,20},{1... | collective-permute-start | bytes 393224 | tf_op jit(solution)/shard_map/ppermute | solution.py:151
  306.2 3.2 collective-permute-start.1
  309.4 20.1 %fusion = f32[4,16,64,256]{3,2,1,0:T(8,128)} fusion(f32[256,4,16,64]{0,3,2,1:T(8,128)S(1)} %bitcast.137, f32[4,16,256]{2,1,0:T(8,128)S(1)} %copy-done.16, f32[4,256,256]{2,1,0:T(8,128)S(1)} %fusion.61, pred[256,256]{1,0:T(8,128)(4,1)S(1)} %copy-done.17), kind=kOutput, calls=%fused_computation | convolution fusion | flops 3238002688 | bytes 9568256 | tf_op jit(solution)/shard_map/while/body/eval_jaxpr/ghts,sghp->tghp/dot_general | solution.py:54
  329.8 1.3 collective-permute-start.13
  331.1 4.4 %collective-permute-start.12 = (f32[1,1,64,512]{3,0,2,1:T(1,128)}, f32[1,1,64,512]{3,0,2,1:T(1,128)}, u32[]{:S(2)}, u32[]{:S(2)}) collective-permute-start(f32[1,1,64,512]{3,0,2,1:T(1,128)} %get-tuple-element.20), channel_id=1, source_target_pairs={{0,24},{2,26},{4,28},{6,30},{8,0},{10,2},{12,4},{14,6},{16,8},{18,... | collective-permute-start | bytes 393224 | tf_op jit(solution)/shard_map/ppermute | solution.py:151
  335.5 5.2 %fusion.29 = f32[4,16,64,256]{3,2,1,0:T(8,128)} fusion(f32[256,4,128,1]{0,2,3,1:T(8,128)S(1)} %bitcast.145), kind=kOutput, calls=%fused_computation.35 | convolution fusion | flops 1610612736 | bytes 4718592 | tf_op jit(solution)/shard_map/while/body/eval_jaxpr/tgn,ghpn->tghp/dot_general | solution.py:58
  340.7 2.3 dynamic_update_slice.48
  343.1 2.3 dynamic_update_slice.49
  345.4 2.3 dynamic_update_slice.50
  347.8 2.3 dynamic_update_slice.51
  350.1 2.3 dynamic_update_slice.52
  352.5 2.3 dynamic_update_slice.53
  354.8 1.1 dynamic_update_slice.54
  356.0 1.1 dynamic_update_slice.55
  357.1 1.1 dynamic_update_slice.56
  358.3 1.1 dynamic_update_slice.57
  359.5 2.3 dynamic_update_slice.58
  361.8 2.3 dynamic_update_slice.59
  364.2 2.3 dynamic_update_slice.60
  366.5 2.3 dynamic_update_slice.61
  368.9 2.3 dynamic_update_slice.62
  371.2 1.4 reshape_reshape.3
  372.7 10.2 %multiply_reduce_fusion = (f32[256,4]{0,1:T(4,128)S(1)}, f32[256,4,16,64]{0,3,2,1:T(8,128)}) fusion(f32[4,16,64,128]{3,2,1,0:T(8,128)} %reshape_reshape.3, f32[256,4,128,1]{0,2,3,1:T(8,128)S(1)} %bitcast.146, f32[256,4,16]{0,2,1:T(8,128)S(1)} %get-tuple-element.47, f32[4,16,64,256]{3,2,1,0:T(8,128)} %fusion.29, f32[4,16,64,256]{3,2,1,0:T(8,128)} %fusion), kind=kOutput, calls=%fused_computation.27 | convolution fusion | flops 1616903168 | bytes 15273984 | tf_op jit(solution)/shard_map/tgn,ghpn->tghp/dot_general | solution.py:157
  382.9 5.8 %copy.74 = f32[256,4096]{1,0:T(8,128)} copy(f32[256,4096]{0,1:T(8,128)} %bitcast.143) | data formatting | bytes 8388608 | tf_op jit(solution)/shard_map/reshape | solution.py:162
  389.5 3.9 copy.89
  393.3 2.6 multiply_multiply_fusion
  (105 shorter events, 8.1 us)
Async XLA Ops:
  1.6 6.3 %all-to-all-start.3 = ((f32[128,2,64]{0,2,1:T(8,128)}), f32[128,2,64]{0,2,1:T(8,128)S(1)}, u32[]{:S(2)}, u32[]{:S(2)}) async-start(f32[128,2,64]{0,2,1:T(8,128)} %bitcast.24), calls=%async_computation.3 | async-start | bytes 131072 | tf_op jit(solution)/shard_map/all_to_all | solution.py:89
  7.8 9.7 %all-to-all-start.1 = ((f32[128,2,512]{0,2,1:T(8,128)}), f32[128,2,512]{0,2,1:T(8,128)S(1)}, u32[]{:S(2)}, u32[]{:S(2)}) async-start(f32[128,2,512]{0,2,1:T(8,128)} %bitcast.4), calls=%async_computation.1 | async-start | bytes 1048576 | tf_op jit(solution)/shard_map/all_to_all | solution.py:87
  17.6 9.1 %all-to-all-start.2 = ((f32[128,2,512]{0,2,1:T(8,128)}), f32[128,2,512]{0,2,1:T(8,128)S(1)}, u32[]{:S(2)}, u32[]{:S(2)}) async-start(f32[128,2,512]{0,2,1:T(8,128)} %bitcast.7), calls=%async_computation.2 | async-start | bytes 1048576 | tf_op jit(solution)/shard_map/all_to_all | solution.py:88
  26.6 5.8 %copy-start.20 = (f32[4,1024]{1,0:T(4,128)S(1)}, f32[4,1024]{1,0:T(4,128)}, u32[]{:S(2)}) copy-start(f32[4,1024]{1,0:T(4,128)} %param.14) | copy-start | bytes 49156
  26.6 5.8 %copy-start.21 = (f32[4,1024]{1,0:T(4,128)S(1)}, f32[4,1024]{1,0:T(4,128)}, u32[]{:S(2)}) copy-start(f32[4,1024]{1,0:T(4,128)} %param.13) | copy-start | bytes 49156
  26.6 5.9 %copy-start.18 = (f32[4,8192]{1,0:T(4,128)S(1)}, f32[4,8192]{1,0:T(4,128)}, u32[]{:S(2)}) copy-start(f32[4,8192]{1,0:T(4,128)} %param.12) | copy-start | bytes 393220
  26.6 49.6 %all-to-all-start = ((f32[128,2,4096]{0,2,1:T(8,128)}), f32[128,2,4096]{0,2,1:T(8,128)}, u32[]{:S(2)}, u32[]{:S(2)}) async-start(f32[128,2,4096]{0,2,1:T(8,128)} %bitcast.139), calls=%async_computation | async-start | bytes 8388608 | tf_op jit(solution)/shard_map/all_to_all | solution.py:86
  82.8 9.0 %collective-permute-start = (f32[3,5120]{1,0:T(4,128)S(1)}, f32[3,5120]{1,0:T(4,128)S(1)}, u32[]{:S(2)}, u32[]{:S(2)}) collective-permute-start(f32[3,5120]{1,0:T(4,128)S(1)} %pad_maximum_fusion.3), channel_id=1, source_target_pairs={{0,2},{2,4},{4,6},{6,8},{8,10},{10,12},{12,14},{14,16},{16,18},{18... | collective-permute-start | bytes 184328 | tf_op jit(solution)/shard_map/ppermute | solution.py:30
  161.3 27.2 %copy-start.22 = (u32[32]{0:T(128)S(1)}, u32[32]{0:T(128)}, u32[]{:S(2)}) copy-start(u32[32]{0:T(128)} %constant.276) | copy-start | bytes 388
  166.8 85.8 %all-to-all-start.4 = ((f32[16,1,32768]{2,1,0:T(1,128)}), f32[16,1,32768]{2,1,0:T(1,128)}, u32[]{:S(2)}, u32[]{:S(2)}) async-start(f32[16,1,32768]{2,1,0:T(1,128)} %reshape.148), calls=%async_computation.4 | async-start | bytes 4194304 | tf_op jit(solution)/shard_map/all_to_all | solution.py:135
  270.6 38.8 %copy-start = (f32[256,4096]{0,1:T(8,128)S(1)}, f32[256,4096]{0,1:T(8,128)}, u32[]{:S(2)}) copy-start(f32[256,4096]{0,1:T(8,128)} %copy.57) | copy-start | bytes 12582916
  270.6 38.8 %copy-start.16 = (f32[4,16,256]{2,1,0:T(8,128)S(1)}, f32[4,16,256]{2,1,0:T(8,128)}, u32[]{:S(2)}) copy-start(f32[4,16,256]{2,1,0:T(8,128)} %get-tuple-element.50) | copy-start | bytes 196612
  270.6 38.8 %copy-start.17 = (pred[256,256]{1,0:T(8,128)(4,1)S(1)}, pred[256,256]{1,0:T(8,128)(4,1)}, u32[]{:S(2)}) copy-start(pred[256,256]{1,0:T(8,128)(4,1)} %iota_compare_fusion) | copy-start | bytes 196612
  277.1 8.9 %collective-permute-start.10 = (f32[1,1,64,512]{3,0,2,1:T(1,128)S(1)}, f32[1,1,64,512]{3,0,2,1:T(1,128)S(1)}, u32[]{:S(2)}, u32[]{:S(2)}) collective-permute-start(f32[1,1,64,512]{3,0,2,1:T(1,128)S(1)} %get-tuple-element.30), channel_id=1, source_target_pairs={{0,20},{2,22},{4,24},{6,26},{8,28},{10,30},{12,0},{14,2},{16,4},{1... | collective-permute-start | bytes 393224 | tf_op jit(solution)/shard_map/ppermute | solution.py:151
  277.2 11.8 %collective-permute-start.9 = (f32[1,1,64,512]{3,0,2,1:T(1,128)S(1)}, f32[1,1,64,512]{3,0,2,1:T(1,128)S(1)}, u32[]{:S(2)}, u32[]{:S(2)}) collective-permute-start(f32[1,1,64,512]{3,0,2,1:T(1,128)S(1)} %get-tuple-element.32), channel_id=1, source_target_pairs={{0,18},{2,20},{4,22},{6,24},{8,26},{10,28},{12,30},{14,0},{16,2},{... | collective-permute-start | bytes 393224 | tf_op jit(solution)/shard_map/ppermute | solution.py:151
  280.1 14.3 %collective-permute-start.8 = (f32[1,1,64,512]{3,0,2,1:T(1,128)S(1)}, f32[1,1,64,512]{3,0,2,1:T(1,128)S(1)}, u32[]{:S(2)}, u32[]{:S(2)}) collective-permute-start(f32[1,1,64,512]{3,0,2,1:T(1,128)S(1)} %get-tuple-element.33), channel_id=1, source_target_pairs={{0,16},{2,18},{4,20},{6,22},{8,24},{10,26},{12,28},{14,30},{16,0},... | collective-permute-start | bytes 393224 | tf_op jit(solution)/shard_map/ppermute | solution.py:151
  281.5 17.4 %collective-permute-start.7 = (f32[1,1,64,512]{3,0,2,1:T(1,128)S(1)}, f32[1,1,64,512]{3,0,2,1:T(1,128)S(1)}, u32[]{:S(2)}, u32[]{:S(2)}) collective-permute-start(f32[1,1,64,512]{3,0,2,1:T(1,128)S(1)} %get-tuple-element.34), channel_id=1, source_target_pairs={{0,14},{2,16},{4,18},{6,20},{8,22},{10,24},{12,26},{14,28},{16,30}... | collective-permute-start | bytes 393224 | tf_op jit(solution)/shard_map/ppermute | solution.py:151
  282.4 23.8 %collective-permute-start.6 = (f32[1,1,64,512]{3,0,2,1:T(1,128)S(1)}, f32[1,1,64,512]{3,0,2,1:T(1,128)S(1)}, u32[]{:S(2)}, u32[]{:S(2)}) collective-permute-start(f32[1,1,64,512]{3,0,2,1:T(1,128)S(1)} %get-tuple-element.35), channel_id=1, source_target_pairs={{0,12},{2,14},{4,16},{6,18},{8,20},{10,22},{12,24},{14,26},{16,28}... | collective-permute-start | bytes 393224 | tf_op jit(solution)/shard_map/ppermute | solution.py:151
  286.1 43.4 %copy-start.2 = (f32[1,1,64,512]{3,0,2,1:T(1,128)}, f32[1,1,64,512]{3,0,2,1:T(1,128)S(1)}, u32[]{:S(2)}) copy-start(f32[1,1,64,512]{3,0,2,1:T(1,128)S(1)} %collective-permute-done.10) | copy-start | bytes 393220
  286.1 43.5 %collective-permute-start.5 = (f32[1,1,64,512]{3,0,2,1:T(1,128)S(1)}, f32[1,1,64,512]{3,0,2,1:T(1,128)S(1)}, u32[]{:S(2)}, u32[]{:S(2)}) collective-permute-start(f32[1,1,64,512]{3,0,2,1:T(1,128)S(1)} %get-tuple-element.36), channel_id=1, source_target_pairs={{0,10},{2,12},{4,14},{6,16},{8,18},{10,20},{12,22},{14,24},{16,26}... | collective-permute-start | bytes 393224 | tf_op jit(solution)/shard_map/ppermute | solution.py:151
  289.0 40.6 %copy-start.4 = (f32[1,1,64,512]{3,0,2,1:T(1,128)}, f32[1,1,64,512]{3,0,2,1:T(1,128)S(1)}, u32[]{:S(2)}) copy-start(f32[1,1,64,512]{3,0,2,1:T(1,128)S(1)} %collective-permute-done.9) | copy-start | bytes 393220
  289.0 40.7 %collective-permute-start.4 = (f32[1,1,64,512]{3,0,2,1:T(1,128)S(1)}, f32[1,1,64,512]{3,0,2,1:T(1,128)S(1)}, u32[]{:S(2)}, u32[]{:S(2)}) collective-permute-start(f32[1,1,64,512]{3,0,2,1:T(1,128)S(1)} %get-tuple-element.37), channel_id=1, source_target_pairs={{0,8},{2,10},{4,12},{6,14},{8,16},{10,18},{12,20},{14,22},{16,24},... | collective-permute-start | bytes 393224 | tf_op jit(solution)/shard_map/ppermute | solution.py:151
  294.5 35.1 %copy-start.6 = (f32[1,1,64,512]{3,0,2,1:T(1,128)}, f32[1,1,64,512]{3,0,2,1:T(1,128)S(1)}, u32[]{:S(2)}) copy-start(f32[1,1,64,512]{3,0,2,1:T(1,128)S(1)} %collective-permute-done.8) | copy-start | bytes 393220
  294.5 35.3 %collective-permute-start.3 = (f32[1,1,64,512]{3,0,2,1:T(1,128)S(1)}, f32[1,1,64,512]{3,0,2,1:T(1,128)S(1)}, u32[]{:S(2)}, u32[]{:S(2)}) collective-permute-start(f32[1,1,64,512]{3,0,2,1:T(1,128)S(1)} %get-tuple-element.38), channel_id=1, source_target_pairs={{0,6},{2,8},{4,10},{6,12},{8,14},{10,16},{12,18},{14,20},{16,22},{... | collective-permute-start | bytes 393224 | tf_op jit(solution)/shard_map/ppermute | solution.py:151
  298.9 30.6 %copy-start.8 = (f32[1,1,64,512]{3,0,2,1:T(1,128)}, f32[1,1,64,512]{3,0,2,1:T(1,128)S(1)}, u32[]{:S(2)}) copy-start(f32[1,1,64,512]{3,0,2,1:T(1,128)S(1)} %collective-permute-done.7) | copy-start | bytes 393220
  298.9 32.1 %collective-permute-start.2 = (f32[1,1,64,512]{3,0,2,1:T(1,128)S(1)}, f32[1,1,64,512]{3,0,2,1:T(1,128)S(1)}, u32[]{:S(2)}, u32[]{:S(2)}) collective-permute-start(f32[1,1,64,512]{3,0,2,1:T(1,128)S(1)} %get-tuple-element.39), channel_id=1, source_target_pairs={{0,4},{2,6},{4,8},{6,10},{8,12},{10,14},{12,16},{14,18},{16,20},{1... | collective-permute-start | bytes 393224 | tf_op jit(solution)/shard_map/ppermute | solution.py:151
  306.2 23.4 %copy-start.10 = (f32[1,1,64,512]{3,0,2,1:T(1,128)}, f32[1,1,64,512]{3,0,2,1:T(1,128)S(1)}, u32[]{:S(2)}) copy-start(f32[1,1,64,512]{3,0,2,1:T(1,128)S(1)} %collective-permute-done.6) | copy-start | bytes 393220
  306.2 29.3 %collective-permute-start.1 = (f32[1,1,64,512]{3,0,2,1:T(1,128)S(1)}, f32[1,1,64,512]{3,0,2,1:T(1,128)S(1)}, u32[]{:S(2)}, u32[]{:S(2)}) collective-permute-start(f32[1,1,64,512]{3,0,2,1:T(1,128)S(1)} %get-tuple-element.40), channel_id=1, source_target_pairs={{0,2},{2,4},{4,6},{6,8},{8,10},{10,12},{12,14},{14,16},{16,18},{18... | collective-permute-start | bytes 393224 | tf_op jit(solution)/shard_map/ppermute | solution.py:151
  329.6 11.1 %copy-start.11 = (f32[1,1,64,512]{3,0,2,1:T(1,128)}, f32[1,1,64,512]{3,0,2,1:T(1,128)S(1)}, u32[]{:S(2)}) copy-start(f32[1,1,64,512]{3,0,2,1:T(1,128)S(1)} %collective-permute-done.5) | copy-start | bytes 393220
  329.6 25.2 %copy-start.9 = (f32[1,1,64,512]{3,0,2,1:T(1,128)S(1)}, f32[1,1,64,512]{3,0,2,1:T(1,128)}, u32[]{:S(2)}) copy-start(f32[1,1,64,512]{3,0,2,1:T(1,128)} %copy-done.8) | copy-start | bytes 393220
  329.6 26.4 %copy-start.7 = (f32[1,1,64,512]{3,0,2,1:T(1,128)S(1)}, f32[1,1,64,512]{3,0,2,1:T(1,128)}, u32[]{:S(2)}) copy-start(f32[1,1,64,512]{3,0,2,1:T(1,128)} %copy-done.6) | copy-start | bytes 393220
  329.6 27.5 %copy-start.5 = (f32[1,1,64,512]{3,0,2,1:T(1,128)S(1)}, f32[1,1,64,512]{3,0,2,1:T(1,128)}, u32[]{:S(2)}) copy-start(f32[1,1,64,512]{3,0,2,1:T(1,128)} %copy-done.4) | copy-start | bytes 393220
  329.6 28.7 %copy-start.3 = (f32[1,1,64,512]{3,0,2,1:T(1,128)S(1)}, f32[1,1,64,512]{3,0,2,1:T(1,128)}, u32[]{:S(2)}) copy-start(f32[1,1,64,512]{3,0,2,1:T(1,128)} %copy-done.2) | copy-start | bytes 393220
  329.6 39.2 %collective-permute-start.15 = (f32[1,1,64,512]{3,0,2,1:T(1,128)S(1)}, f32[1,1,64,512]{3,0,2,1:T(1,128)}, u32[]{:S(2)}, u32[]{:S(2)}) collective-permute-start(f32[1,1,64,512]{3,0,2,1:T(1,128)S(1)} %get-tuple-element.17), channel_id=1, source_target_pairs={{0,30},{2,0},{4,2},{6,4},{8,6},{10,8},{12,10},{14,12},{16,14},{18,... | collective-permute-start | bytes 393224 | tf_op jit(solution)/shard_map/ppermute | solution.py:151
  329.7 11.0 %copy-start.12 = (f32[1,1,64,512]{3,0,2,1:T(1,128)}, f32[1,1,64,512]{3,0,2,1:T(1,128)S(1)}, u32[]{:S(2)}) copy-start(f32[1,1,64,512]{3,0,2,1:T(1,128)S(1)} %collective-permute-done.4) | copy-start | bytes 393220
  329.7 36.8 %collective-permute-start.14 = (f32[1,1,64,512]{3,0,2,1:T(1,128)S(1)}, f32[1,1,64,512]{3,0,2,1:T(1,128)}, u32[]{:S(2)}, u32[]{:S(2)}) collective-permute-start(f32[1,1,64,512]{3,0,2,1:T(1,128)S(1)} %get-tuple-element.18), channel_id=1, source_target_pairs={{0,28},{2,30},{4,0},{6,2},{8,4},{10,6},{12,8},{14,10},{16,12},{18,... | collective-permute-start | bytes 393224 | tf_op jit(solution)/shard_map/ppermute | solution.py:151
  329.8 10.9 %copy-start.13 = (f32[1,1,64,512]{3,0,2,1:T(1,128)}, f32[1,1,64,512]{3,0,2,1:T(1,128)S(1)}, u32[]{:S(2)}) copy-start(f32[1,1,64,512]{3,0,2,1:T(1,128)S(1)} %collective-permute-done.3) | copy-start | bytes 393220
  329.8 34.4 %collective-permute-start.13 = (f32[1,1,64,512]{3,0,2,1:T(1,128)}, f32[1,1,64,512]{3,0,2,1:T(1,128)}, u32[]{:S(2)}, u32[]{:S(2)}) collective-permute-start(f32[1,1,64,512]{3,0,2,1:T(1,128)} %get-tuple-element.19), channel_id=1, source_target_pairs={{0,26},{2,28},{4,30},{6,0},{8,2},{10,4},{12,6},{14,8},{16,10},{18,... | collective-permute-start | bytes 393224 | tf_op jit(solution)/shard_map/ppermute | solution.py:151
  331.1 9.6 %copy-start.14 = (f32[1,1,64,512]{3,0,2,1:T(1,128)}, f32[1,1,64,512]{3,0,2,1:T(1,128)S(1)}, u32[]{:S(2)}) copy-start(f32[1,1,64,512]{3,0,2,1:T(1,128)S(1)} %collective-permute-done.2) | copy-start | bytes 393220
  331.1 30.7 %collective-permute-start.12 = (f32[1,1,64,512]{3,0,2,1:T(1,128)}, f32[1,1,64,512]{3,0,2,1:T(1,128)}, u32[]{:S(2)}, u32[]{:S(2)}) collective-permute-start(f32[1,1,64,512]{3,0,2,1:T(1,128)} %get-tuple-element.20), channel_id=1, source_target_pairs={{0,24},{2,26},{4,28},{6,30},{8,0},{10,2},{12,4},{14,6},{16,8},{18,... | collective-permute-start | bytes 393224 | tf_op jit(solution)/shard_map/ppermute | solution.py:151
  335.5 5.2 %copy-start.15 = (f32[1,1,64,512]{3,0,2,1:T(1,128)}, f32[1,1,64,512]{3,0,2,1:T(1,128)S(1)}, u32[]{:S(2)}) copy-start(f32[1,1,64,512]{3,0,2,1:T(1,128)S(1)} %collective-permute-done.1) | copy-start | bytes 393220
  335.5 24.0 %collective-permute-start.11 = (f32[1,1,64,512]{3,0,2,1:T(1,128)}, f32[1,1,64,512]{3,0,2,1:T(1,128)}, u32[]{:S(2)}, u32[]{:S(2)}) collective-permute-start(f32[1,1,64,512]{3,0,2,1:T(1,128)} %get-tuple-element.28), channel_id=1, source_target_pairs={{0,22},{2,24},{4,26},{6,28},{8,30},{10,0},{12,2},{14,4},{16,6},{18... | collective-permute-start | bytes 393224 | tf_op jit(solution)/shard_map/ppermute | solution.py:151
  389.4 3.9 copy-start.1
  389.4 3.9 copy-start.19
